TPU v7x, 128 devices: a whole 4x4x4 slice. The times are simulated.
128 devices in a mesh: wide: 32 (over y, z_lo, x), narrow: 4 (over z_hi, core).
Axes of the slice: x: 4, y: 4, z: 4 (z_hi: 2, z_lo: 2; z = z_hi * 2 + z_lo), core: 2. Of those that a mesh axis runs over, the one named last changes fastest.
Arguments:
- loads: float32 [98304, 512], P('wide', 'narrow'), may hold values from -6 to 6
- start: float32 [98304, 512], P('wide', 'narrow'), may hold values from -6 to 6
- stiffness: bfloat16 [128, 1024, 1024], P('wide')
- local_inverse: bfloat16 [128, 1024, 1024], P('wide')
- modes: bfloat16 [128, 1024, 32], P('wide'), may hold values from -0.1875 to 0.1875
- coarse_inverse: float32 [4096, 4096], P('wide', 'narrow'), as said below
- margin_rows: int32 [128, 256], P('wide'), may hold values from 0 to 98303, as said below
Outputs:
- displacement: float32 [98304, 512], P('wide', 'narrow')
- final_residual: float32 [98304, 512], P('wide', 'narrow')
Inputs may be any that keep to these rules, and one draw needn't show every extreme that they name: Row s lists 256 distinct rows of loads, none of them rows s * 768 to s * 768 + 767. Call rows i * 4 * 768 to (i + 1) * 4 * 768 - 1 block i. For every i, the entries of rows i * 4 to (i + 1) * 4 - 1 of margin_rows fall at most 48 times into any one block, and exactly 48 times into some block. coarse_inverse equals its transpose.
All inputs are finite; a program needn't handle non-finite values.
Results may differ from a plain program's by a relative error of at most 0.0062.
Values may be sent and summed in bfloat16 or wider, within the bound.
A program may use at most 128 MiB of HBM per device.

v0:
```python
import jax
import jax.numpy as jnp
from jax import lax
from jax.sharding import PartitionSpec as P

ITERS = 2
damping = 0.5


def apply_each(matrices, vectors):
    return jnp.einsum("sij,sjc->sic", matrices, vectors, preferred_element_type=jnp.float32)


def shards(loads, start, stiffness, local_inverse, modes, coarse_inverse, margin_rows):
    owners = lax.axis_size("wide")
    sub_count, margin_count = margin_rows.shape
    matrix_order = stiffness.shape[1]
    core_count = matrix_order - margin_count
    held_rows, col_count = loads.shape
    mode_count = modes.shape[2]
    coarse_rows_dev = sub_count * mode_count
    capacity = 3 * sub_count * margin_count // (2 * owners)
    flat_rows = margin_rows.reshape(-1)
    source = flat_rows // held_rows
    remote_row = flat_rows - source * held_rows
    onehot = (source[:, None] == jnp.arange(owners, dtype=jnp.int32)[None, :]).astype(jnp.int32)
    before = jnp.cumsum(onehot, axis=0) - onehot
    placed = source * capacity + jnp.sum(before * onehot, axis=1)
    requested = jnp.full((owners * capacity,), -1, jnp.int32).at[placed].set(remote_row)
    wanted = lax.all_to_all(
        requested.reshape(owners, capacity), "wide", split_axis=0, concat_axis=0, tiled=True
    )
    usable = (wanted >= 0).reshape(-1)
    picked = jnp.where(usable, wanted.reshape(-1), 0)

    def gather_local(field):
        field_low = field.astype(jnp.bfloat16)
        outgoing = jnp.where(usable[:, None], field_low[picked], jnp.zeros((), jnp.bfloat16))
        incoming = lax.all_to_all(
            outgoing.reshape(owners, capacity, col_count),
            "wide",
            split_axis=0,
            concat_axis=0,
            tiled=True,
        )
        outer_part = incoming.reshape(owners * capacity, col_count)[placed].reshape(
            sub_count, margin_count, col_count
        )
        core_part = field_low.reshape(sub_count, core_count, col_count)
        return jnp.concatenate([core_part, outer_part], axis=1)

    def assemble_parts(parts):
        outer_part = parts[:, core_count:, :].reshape(sub_count * margin_count, col_count)
        outgoing = jnp.zeros((owners * capacity, col_count), jnp.float32).at[placed].set(outer_part)
        incoming = lax.all_to_all(
            outgoing.reshape(owners, capacity, col_count),
            "wide",
            split_axis=0,
            concat_axis=0,
            tiled=True,
        )
        summed = parts[:, :core_count, :].reshape(held_rows, col_count)
        return summed.at[picked].add(incoming.reshape(owners * capacity, col_count))

    def residual_of(field):
        return loads - assemble_parts(apply_each(stiffness, gather_local(field)))

    field = start
    for iteration in range(ITERS):
        residual = residual_of(field)
        restricted = gather_local(residual)
        solved_local = apply_each(local_inverse, restricted)
        projection = jnp.einsum(
            "sim,sic->smc", modes, restricted, preferred_element_type=jnp.float32
        )
        solve_projection = projection.reshape(coarse_rows_dev, col_count)
        gathered = lax.all_gather(solve_projection, "wide", axis=0, tiled=True)
        tile_width = coarse_inverse.shape[1]
        row_offset = lax.axis_index("narrow") * tile_width
        selected = lax.dynamic_slice_in_dim(
            lax.all_gather(gathered, "narrow", axis=1, tiled=True), row_offset, tile_width, 0
        )
        partial_sums = jnp.dot(coarse_inverse, selected, precision=lax.Precision.HIGHEST)
        coarse = lax.psum_scatter(partial_sums, "narrow", scatter_dimension=1, tiled=True)
        lifted = jnp.einsum(
            "sim,smc->sic",
            modes.astype(jnp.float32),
            coarse.reshape(sub_count, mode_count, col_count),
            precision=lax.Precision.HIGHEST,
        )
        change = assemble_parts(damping * solved_local + lifted)
        field = field + change
    return (field, residual_of(field))


def solution(mesh):
    placed = (
        P("wide", "narrow"),
        P("wide", "narrow"),
        P("wide", None, None),
        P("wide", None, None),
        P("wide", None, None),
        P("wide", "narrow"),
        P("wide", None),
    )
    return jax.shard_map(
        shards,
        mesh=mesh,
        in_specs=placed,
        out_specs=(P("wide", "narrow"), P("wide", "narrow")),
        check_vma=False,
    )
```

profile of v0, /device:TPU:0, one launch (start us, length us, event | category | flops | bytes accessed | tf_op | source)
XLA Modules:
  0.0 880.2 jit_solution(7259748184903397401)
XLA Ops:
  10.8 9.0 %reduce-window.6 = s32[32,8,128]{2,1,0:T(8,128)S(1)} reduce-window(s32[32,8,128]{2,1,0:T(8,128)S(1)} %fusion.34, s32[]{:T(128)} %constant.15.clone.1), window={size=1x1x128 pad=0_0x0_0x127_0}, to_apply=%region_0.1 | reduce-window | flops 4161536 | bytes 262148 | tf_op jit(solution)/shard_map/reduce-window
  25.4 8.8 all-to-all-start
  35.6 6.7 all-to-all-done
  52.2 9.4 %all-to-all-done.1 = bf16[32,48,128]{2,1,0:T(8,128)(2,1)S(1)} async-done(((bf16[32,48,128]{2,1,0:T(8,128)(2,1)}), bf16[32,48,128]{2,1,0:T(8,128)(2,1)S(1)}, u32[]{:S(2)}, u32[]{:S(2)}) %all-to-all-start.1) | async-done | bytes 393248 | tf_op jit(solution)/shard_map/all_to_all | solution.py:39
  65.6 6.4 convolution_bitcast_fusion.2
  84.6 8.8 %all-to-all-done.2 = f32[32,48,128]{2,1,0:T(8,128)S(1)} async-done(((f32[32,48,128]{2,1,0:T(8,128)}), f32[32,48,128]{2,1,0:T(8,128)S(1)}, u32[]{:S(2)}, u32[]{:S(2)}) %all-to-all-start.2) | async-done | bytes 786464 | tf_op jit(solution)/shard_map/all_to_all | solution.py:55
  93.4 9.5 %scatter_fusion = f32[3072,128]{1,0:T(8,128)S(1)} fusion(f32[3072,128]{1,0:T(8,128)S(1)} %bitcast.119, s32[1536]{0:T(1024)S(1)} %fusion.35, f32[1536,128]{1,0:T(8,128)S(1)} %bitcast.132), kind=kCustom, calls=%fused_computation.12 | custom fusion | flops 196608 | bytes 2365440 | tf_op jit(solution)/shard_map/scatter-add | solution.py:63
  113.6 9.2 %all-to-all-done.3 = bf16[32,48,128]{2,1,0:T(8,128)(2,1)S(1)} async-done(((bf16[32,48,128]{2,1,0:T(8,128)(2,1)}), bf16[32,48,128]{2,1,0:T(8,128)(2,1)S(1)}, u32[]{:S(2)}, u32[]{:S(2)}) %all-to-all-start.3) | async-done | bytes 393248 | tf_op jit(solution)/shard_map/all_to_all | solution.py:39
  127.3 151.5 %all-gather.5.cloned.1.call-done = f32[4096,128]{1,0:T(8,128)} async-done(((f32[128,128]{1,0:T(8,128)}), f32[4096,128]{1,0:T(8,128)}) %all-gather.5.cloned.1.call-update) | async-done | bytes 2097168 | tf_op jit(solution)/shard_map/all_gather | solution.py:77
  278.9 65.2 %all-gather.7.cloned.1.call-done = f32[4096,512]{1,0:T(8,128)} async-done(((f32[4096,128]{1,0:T(8,128)}), f32[4096,512]{1,0:T(8,128)}) %all-gather.7.cloned.1.call-update) | async-done | bytes 8388624 | tf_op jit(solution)/shard_map/all_gather | solution.py:81
  344.1 5.7 fusion.4
  349.8 26.5 %reduce-scatter.3.cloned.1.call-done = f32[128,128]{0,1:T(8,128)} async-done(((f32[128,512]{0,1:T(8,128)}), f32[128,128]{0,1:T(8,128)}) %reduce-scatter.3.cloned.1.call-update) | async-done | bytes 65552 | tf_op jit(solution)/shard_map/reduce_scatter | solution.py:84
  378.3 6.3 add_bitcast_fusion.1
  390.7 7.2 all-to-all-start.4
  399.9 12.1 %all-to-all-done.4 = f32[32,48,128]{2,1,0:T(8,128)S(1)} async-done(((f32[32,48,128]{2,1,0:T(8,128)}), f32[32,48,128]{2,1,0:T(8,128)S(1)}, u32[]{:S(2)}, u32[]{:S(2)}) %all-to-all-start.4) | async-done | bytes 786464 | tf_op jit(solution)/shard_map/all_to_all | solution.py:55
  412.0 9.7 %scatter_fusion.1 = f32[3072,128]{1,0:T(8,128)S(1)} fusion(f32[3072,128]{1,0:T(8,128)S(1)} %bitcast_add_fusion.1, s32[1536]{0:T(1024)S(1)} %fusion.35, f32[1536,128]{1,0:T(8,128)S(1)} %bitcast.135), kind=kCustom, calls=%fused_computation.14 | custom fusion | flops 196608 | bytes 2365440 | tf_op jit(solution)/shard_map/scatter-add | solution.py:63
  432.3 8.5 all-to-all-done.5
  446.6 6.3 convolution_bitcast_fusion.1
  468.3 5.9 all-to-all-done.6
  474.2 10.8 %scatter_fusion.2 = f32[3072,128]{1,0:T(8,128)} fusion(f32[3072,128]{1,0:T(8,128)} %bitcast.120, s32[1536]{0:T(1024)S(1)} %fusion.35, f32[1536,128]{1,0:T(8,128)S(1)} %bitcast.133), kind=kCustom, calls=%fused_computation.16 | custom fusion | flops 196608 | bytes 2365440 | tf_op jit(solution)/shard_map/scatter-add | solution.py:63
  497.7 8.5 all-to-all-done.7
  513.1 149.8 %all-gather.9.cloned.1.call-done = f32[4096,128]{1,0:T(8,128)} async-done(((f32[128,128]{1,0:T(8,128)}), f32[4096,128]{1,0:T(8,128)}) %all-gather.9.cloned.1.call-update) | async-done | bytes 2097168 | tf_op jit(solution)/shard_map/all_gather | solution.py:77
  663.4 64.8 %all-gather.11.cloned.1.call-done = f32[4096,512]{1,0:T(8,128)} async-done(((f32[4096,128]{1,0:T(8,128)}), f32[4096,512]{1,0:T(8,128)}) %all-gather.11.cloned.1.call-update) | async-done | bytes 8388624 | tf_op jit(solution)/shard_map/all_gather | solution.py:81
  733.8 26.4 %reduce-scatter.5.cloned.1.call-done = f32[128,128]{0,1:T(8,128)} async-done(((f32[128,512]{0,1:T(8,128)}), f32[128,128]{0,1:T(8,128)}) %reduce-scatter.5.cloned.1.call-update) | async-done | bytes 65552 | tf_op jit(solution)/shard_map/reduce_scatter | solution.py:84
  762.3 6.3 add_bitcast_fusion
  777.2 7.2 all-to-all-start.8
  787.1 11.5 %all-to-all-done.8 = f32[32,48,128]{2,1,0:T(8,128)S(1)} async-done(((f32[32,48,128]{2,1,0:T(8,128)}), f32[32,48,128]{2,1,0:T(8,128)S(1)}, u32[]{:S(2)}, u32[]{:S(2)}) %all-to-all-start.8) | async-done | bytes 786464 | tf_op jit(solution)/shard_map/all_to_all | solution.py:55
  798.6 10.8 %scatter_fusion.3 = f32[3072,128]{1,0:T(8,128)} fusion(f32[3072,128]{1,0:T(8,128)} %bitcast_add_fusion, s32[1536]{0:T(1024)S(1)} %fusion.35, f32[1536,128]{1,0:T(8,128)S(1)} %bitcast.134), kind=kCustom, calls=%fused_computation.18 | custom fusion | flops 196608 | bytes 2365440 | tf_op jit(solution)/shard_map/scatter-add | solution.py:63
  820.1 9.4 %all-to-all-done.9 = bf16[32,48,128]{2,1,0:T(8,128)(2,1)S(1)} async-done(((bf16[32,48,128]{2,1,0:T(8,128)(2,1)}), bf16[32,48,128]{2,1,0:T(8,128)(2,1)S(1)}, u32[]{:S(2)}, u32[]{:S(2)}) %all-to-all-start.9) | async-done | bytes 393248 | tf_op jit(solution)/shard_map/all_to_all | solution.py:39
  833.6 6.4 convolution_bitcast_fusion
  852.6 8.5 all-to-all-done.10
  861.0 9.5 %scatter_fusion.4 = f32[3072,128]{1,0:T(8,128)S(1)} fusion(f32[3072,128]{1,0:T(8,128)S(1)} %bitcast.118, s32[1536]{0:T(1024)S(1)} %fusion.35, f32[1536,128]{1,0:T(8,128)S(1)} %bitcast.131), kind=kCustom, calls=%fused_computation.20 | custom fusion | flops 196608 | bytes 2365440 | tf_op jit(solution)/shard_map/scatter-add | solution.py:63
  (136 shorter events, 162.9 us)
Async XLA Ops:
  7.2 336.9 %copy-start = (f32[128,1024]{1,0:T(8,128)S(1)}, f32[128,1024]{1,0:T(8,128)}, u32[]{:S(2)}) copy-start(f32[128,1024]{1,0:T(8,128)} %param.12) | copy-start | bytes 1572868
  20.3 52.7 %copy-start.10 = (s32[1024,1]{0,1:T(1,128)}, s32[1024,1]{0,1:T(1,128)S(1)}, u32[]{:S(2)}) copy-start(s32[1024,1]{0,1:T(1,128)S(1)} %compare_select_fusion.2) | copy-start | bytes 12292
  25.4 17.0 %all-to-all-start = ((s32[32,1,48]{2,1,0:T(1,128)}), s32[32,1,48]{2,1,0:T(1,128)S(1)}, u32[]{:S(2)}, u32[]{:S(2)}) async-start(s32[32,1,48]{2,1,0:T(1,128)} %all_to_all.38), calls=%async_computation | async-start | bytes 32768 | tf_op jit(solution)/shard_map/all_to_all | solution.py:30
  42.4 65.3 %copy-start.5 = (pred[32,48]{1,0:T(8,128)(4,1)}, pred[32,48]{1,0:T(8,128)(4,1)S(1)}, u32[]{:S(2)}) copy-start(pred[32,48]{1,0:T(8,128)(4,1)S(1)} %compare_bitcast_fusion) | copy-start | bytes 4612
  48.0 13.6 %all-to-all-start.1 = ((bf16[32,48,128]{2,1,0:T(8,128)(2,1)}), bf16[32,48,128]{2,1,0:T(8,128)(2,1)S(1)}, u32[]{:S(2)}, u32[]{:S(2)}) async-start(bf16[32,48,128]{2,1,0:T(8,128)(2,1)} %broadcast_select_fusion.4), calls=%async_computation.1 | async-start | bytes 786432 | tf_op jit(solution)/shard_map/all_to_all | solution.py:39
  52.1 19.8 %copy-start.7 = (s32[1024]{0:T(1024)}, s32[1024]{0:T(1024)S(1)}, u32[]{:S(2)}) copy-start(s32[1024]{0:T(1024)S(1)} %broadcast_clamp_fusion) | copy-start | bytes 12292
  77.4 16.0 %all-to-all-start.2 = ((f32[32,48,128]{2,1,0:T(8,128)}), f32[32,48,128]{2,1,0:T(8,128)S(1)}, u32[]{:S(2)}, u32[]{:S(2)}) async-start(f32[32,48,128]{2,1,0:T(8,128)} %bitcast.137), calls=%async_computation.2 | async-start | bytes 1572864 | tf_op jit(solution)/shard_map/all_to_all | solution.py:55
  107.6 15.2 %copy-start.8 = (s32[1024]{0:T(1024)S(1)}, s32[1024]{0:T(1024)}, u32[]{:S(2)}) copy-start(s32[1024]{0:T(1024)} %copy-done.7) | copy-start | bytes 12292
  108.7 14.1 %all-to-all-start.3 = ((bf16[32,48,128]{2,1,0:T(8,128)(2,1)}), bf16[32,48,128]{2,1,0:T(8,128)(2,1)S(1)}, u32[]{:S(2)}, u32[]{:S(2)}) async-start(bf16[32,48,128]{2,1,0:T(8,128)(2,1)} %broadcast_select_fusion.3), calls=%async_computation.3 | async-start | bytes 786432 | tf_op jit(solution)/shard_map/all_to_all | solution.py:39
  113.1 165.7 %all-gather.5.cloned.1.call-start = ((), (), s32[]{:S(2)}) async-start(), calls=%async_computation.13 | async-start | bytes 2162688 | tf_op jit(solution)/shard_map/all_gather | solution.py:77
  113.3 12.9 %copy-start.4 = (bf16[4,1024,32]{1,2,0:T(8,128)(2,1)S(1)}, bf16[4,1024,32]{1,2,0:T(8,128)(2,1)}, u32[]{:S(2)}) copy-start(bf16[4,1024,32]{1,2,0:T(8,128)(2,1)} %param.11) | copy-start | bytes 786436
  127.3 216.8 %all-gather.7.cloned.1.call-start = ((), (), s32[]{:S(2)}) async-start(), calls=%async_computation.14 | async-start | bytes 10485760 | tf_op jit(solution)/shard_map/all_gather | solution.py:81
  278.8 97.5 %reduce-scatter.3.cloned.1.call-start = ((), (), s32[]{:S(2)}) async-start(), calls=%async_computation.15 | async-start | bytes 327680 | tf_op jit(solution)/shard_map/reduce_scatter | solution.py:84
  390.7 21.4 %all-to-all-start.4 = ((f32[32,48,128]{2,1,0:T(8,128)}), f32[32,48,128]{2,1,0:T(8,128)S(1)}, u32[]{:S(2)}, u32[]{:S(2)}) async-start(f32[32,48,128]{2,1,0:T(8,128)} %bitcast.26), calls=%async_computation.5 | async-start | bytes 1572864 | tf_op jit(solution)/shard_map/all_to_all | solution.py:55
  426.7 14.1 %all-to-all-start.5 = ((bf16[32,48,128]{2,1,0:T(8,128)(2,1)}), bf16[32,48,128]{2,1,0:T(8,128)(2,1)S(1)}, u32[]{:S(2)}, u32[]{:S(2)}) async-start(bf16[32,48,128]{2,1,0:T(8,128)(2,1)} %broadcast_select_fusion.2), calls=%async_computation.6 | async-start | bytes 786432 | tf_op jit(solution)/shard_map/all_to_all | solution.py:39
  432.3 14.3 %copy-start.2 = (bf16[4,768,128]{1,2,0:T(8,128)(2,1)S(1)}, bf16[4,768,128]{1,2,0:T(8,128)(2,1)}, u32[]{:S(2)}) copy-start(bf16[4,768,128]{1,2,0:T(8,128)(2,1)} %copy.78) | copy-start | bytes 2359300
  452.8 1.3 copy-start.1
  458.5 15.6 %all-to-all-start.6 = ((f32[32,48,128]{2,1,0:T(8,128)}), f32[32,48,128]{2,1,0:T(8,128)S(1)}, u32[]{:S(2)}, u32[]{:S(2)}) async-start(f32[32,48,128]{2,1,0:T(8,128)} %bitcast.138), calls=%async_computation.7 | async-start | bytes 1572864 | tf_op jit(solution)/shard_map/all_to_all | solution.py:55
  491.9 14.2 %all-to-all-start.7 = ((bf16[32,48,128]{2,1,0:T(8,128)(2,1)}), bf16[32,48,128]{2,1,0:T(8,128)(2,1)S(1)}, u32[]{:S(2)}, u32[]{:S(2)}) async-start(bf16[32,48,128]{2,1,0:T(8,128)(2,1)} %broadcast_select_fusion.1), calls=%async_computation.8 | async-start | bytes 786432 | tf_op jit(solution)/shard_map/all_to_all | solution.py:39
  496.4 166.4 %all-gather.9.cloned.1.call-start = ((), (), s32[]{:S(2)}) async-start(), calls=%async_computation.16 | async-start | bytes 2162688 | tf_op jit(solution)/shard_map/all_gather | solution.py:77
  497.7 14.2 %copy-start.3 = (bf16[4,768,128]{1,2,0:T(8,128)(2,1)S(1)}, bf16[4,768,128]{1,2,0:T(8,128)(2,1)}, u32[]{:S(2)}) copy-start(bf16[4,768,128]{1,2,0:T(8,128)(2,1)} %copy.82) | copy-start | bytes 2359300
  513.0 215.1 %all-gather.11.cloned.1.call-start = ((), (), s32[]{:S(2)}) async-start(), calls=%async_computation.17 | async-start | bytes 10485760 | tf_op jit(solution)/shard_map/all_gather | solution.py:81
  662.9 97.4 %reduce-scatter.5.cloned.1.call-start = ((), (), s32[]{:S(2)}) async-start(), calls=%async_computation.18 | async-start | bytes 327680 | tf_op jit(solution)/shard_map/reduce_scatter | solution.py:84
  777.2 21.4 %all-to-all-start.8 = ((f32[32,48,128]{2,1,0:T(8,128)}), f32[32,48,128]{2,1,0:T(8,128)S(1)}, u32[]{:S(2)}, u32[]{:S(2)}) async-start(f32[32,48,128]{2,1,0:T(8,128)} %bitcast.139), calls=%async_computation.10 | async-start | bytes 1572864 | tf_op jit(solution)/shard_map/all_to_all | solution.py:55
  810.9 3.2 copy-start.6
  814.1 15.4 %copy-start.9 = (s32[1024]{0:T(1024)S(1)}, s32[1024]{0:T(1024)}, u32[]{:S(2)}) copy-start(s32[1024]{0:T(1024)} %copy-done.7) | copy-start | bytes 12292
  815.2 14.4 %all-to-all-start.9 = ((bf16[32,48,128]{2,1,0:T(8,128)(2,1)}), bf16[32,48,128]{2,1,0:T(8,128)(2,1)S(1)}, u32[]{:S(2)}, u32[]{:S(2)}) async-start(bf16[32,48,128]{2,1,0:T(8,128)(2,1)} %broadcast_select_fusion), calls=%async_computation.11 | async-start | bytes 786432 | tf_op jit(solution)/shard_map/all_to_all | solution.py:39
  845.4 15.6 %all-to-all-start.10 = ((f32[32,48,128]{2,1,0:T(8,128)}), f32[32,48,128]{2,1,0:T(8,128)S(1)}, u32[]{:S(2)}, u32[]{:S(2)}) async-start(f32[32,48,128]{2,1,0:T(8,128)} %bitcast.136), calls=%async_computation.12 | async-start | bytes 1572864 | tf_op jit(solution)/shard_map/all_to_all | solution.py:55
Sparse Core Ops, SparseCore 0:
  127.4 151.3 all-gather.4
  280.4 63.5 all-gather.6
  349.9 26.2 reduce-scatter.2
  513.1 149.6 all-gather.8
  664.5 63.5 all-gather.10
  734.0 26.2 reduce-scatter.4
where the time goes:
time: 891 us; the launch traced here: 880 us
  waiting for transfers between devices  583 us (65%)
  local copies, waits for them, and re-layouts  93.7 us (11%)
  other arithmetic  83.6 us (9%)
  starting transfers between devices  57.9 us (6%)
  matrix products  47.3 us (5%)
  between operations  14.9 us (2%)
    all_gather x2, waiting for transfers between devices, shards(): gathered = lax.all_gather(solve_projection, 'wide', axis=0, tiled=True)  301 us
    all_gather x2, waiting for transfers between devices, shards(): lax.all_gather(gathered, 'narrow', axis=1, tiled=True)  130 us
    reduce_scatter x2, waiting for transfers between devices, shards(): lax.psum_scatter(partial_sums, 'narrow', scatter_dimension=1, tiled=True)  52.9 us
    scatter-add x5, other arithmetic, assemble_parts(): return summed.at[picked].add(incoming.reshape(owners * capacity, col_count))  50.2 us
    all_to_all x5, waiting for transfers between devices, assemble_parts(): lax.all_to_all(outgoing.reshape(owners, capacity, col_count), 'wide', spl...  46.7 us
    all_to_all x5, waiting for transfers between devices, gather_local(): lax.all_to_all(outgoing.reshape(owners, capacity, col_count), 'wide', spl...  45.1 us
    dot_general x5, matrix products, apply_each(): jnp.einsum('sij,sjc->sic', matrices, vectors, preferred_element_type=jnp....  31.6 us
    all_to_all x5, starting transfers between devices, assemble_parts(): lax.all_to_all(outgoing.reshape(owners, capacity, col_count), 'wide', spl...  26.4 us
  transfers between devices with their start and end apart: 17, of which 17 were waited for; matrix products, arithmetic and copies ran while one was open for 2% of the time, Pallas kernels for 0%

commit v1 on v0

--- a/solution.py
+++ b/solution.py
@@ -78,7 +78,13 @@
         tile_width = coarse_inverse.shape[1]
         row_offset = lax.axis_index("narrow") * tile_width
         selected = lax.dynamic_slice_in_dim(
-            lax.all_gather(gathered, "narrow", axis=1, tiled=True), row_offset, tile_width, 0
+            jnp.concatenate(
+                lax.all_to_all(jnp.stack([gathered] * lax.axis_size("narrow")), "narrow", 0, 0),
+                axis=1,
+            ),
+            row_offset,
+            tile_width,
+            0,
         )
         partial_sums = jnp.dot(coarse_inverse, selected, precision=lax.Precision.HIGHEST)
         coarse = lax.psum_scatter(partial_sums, "narrow", scatter_dimension=1, tiled=True)

time: 891 us -> 965 us (1.083)
  blocking collectives: 0 us -> 98.9 us
  waiting for transfers between devices: 583 us -> 546 us
  local copies, waits for them, and re-layouts: 93.7 us -> 106 us
    all_gather x2 -> x0, waiting for transfers between devices: 130 us -> none  [shards(): lax.all_gather(gathered, 'narrow', axis=1, tiled=True)]
    all_to_all x0 -> x1, blocking collectives: none -> 98.9 us  [shards(): lax.all_to_all(jnp.stack([gathered] * lax.axis_size('narrow')), 'narrow',...]
    all_to_all x0 -> x1, waiting for transfers between devices: none -> 94.6 us  [shards(): lax.all_to_all(jnp.stack([gathered] * lax.axis_size('narrow')), 'narrow',...]
  transfers between devices with their start and end apart: 17 -> 16, of which waited for: 17 -> 16; matrix products, arithmetic and copies ran while one was open for 2% -> 2% of each run, Pallas kernels for 0% -> 0%
where the time goes in v1:
time: 965 us; the launch traced here: 954 us
  waiting for transfers between devices  546 us (57%)
  local copies, waits for them, and re-layouts  106 us (11%)
  blocking collectives  98.9 us (10%)
  other arithmetic  83.4 us (9%)
  starting transfers between devices  63.3 us (7%)
  matrix products  42.5 us (4%)
  between operations  14.6 us (2%)
    all_gather x2, waiting for transfers between devices, shards(): gathered = lax.all_gather(solve_projection, 'wide', axis=0, tiled=True)  301 us
    all_to_all x1, blocking collectives, shards(): lax.all_to_all(jnp.stack([gathered] * lax.axis_size('narrow')), 'narrow',...  98.9 us
    all_to_all x1, waiting for transfers between devices, shards(): lax.all_to_all(jnp.stack([gathered] * lax.axis_size('narrow')), 'narrow',...  94.6 us
    reduce_scatter x2, waiting for transfers between devices, shards(): lax.psum_scatter(partial_sums, 'narrow', scatter_dimension=1, tiled=True)  51.1 us
    scatter-add x5, other arithmetic, assemble_parts(): return summed.at[picked].add(incoming.reshape(owners * capacity, col_count))  50 us
    all_to_all x5, waiting for transfers between devices, assemble_parts(): lax.all_to_all(outgoing.reshape(owners, capacity, col_count), 'wide', spl...  46.7 us
    all_to_all x5, waiting for transfers between devices, gather_local(): lax.all_to_all(outgoing.reshape(owners, capacity, col_count), 'wide', spl...  45 us
    dot_general x5, matrix products, apply_each(): jnp.einsum('sij,sjc->sic', matrices, vectors, preferred_element_type=jnp....  31.6 us
  transfers between devices with their start and end apart: 16, of which 16 were waited for; matrix products, arithmetic and copies ran while one was open for 2% of the time, Pallas kernels for 0%

profile of v1, /device:TPU:0, one launch (start us, length us, event | category | flops | bytes accessed | tf_op | source)
XLA Modules:
  0.0 953.9 jit_solution(1060679815799019603)
XLA Ops:
  10.8 9.0 reduce-window.6
  25.4 8.8 all-to-all-start
  35.6 6.7 all-to-all-done
  52.2 9.4 all-to-all-done.1
  65.6 6.4 convolution_bitcast_fusion.2
  84.6 8.8 all-to-all-done.2
  93.4 9.5 scatter_fusion
  113.6 9.2 all-to-all-done.3
  127.3 151.5 %all-gather.3.cloned.1.call-done = f32[4096,128]{1,0:T(8,128)} async-done(((f32[128,128]{1,0:T(8,128)}), f32[4096,128]{1,0:T(8,128)}) %all-gather.3.cloned.1.call-update) | async-done | bytes 2097168 | tf_op jit(solution)/shard_map/all_gather | solution.py:77
  285.1 5.6 all-to-all-start.4
  290.8 94.6 %all-to-all-done.4 = f32[4,4096,128]{1,2,0:T(8,128)} async-done(((f32[4,4096,128]{1,2,0:T(8,128)}), f32[4,4096,128]{1,2,0:T(8,128)}, u32[]{:S(2)}, u32[]{:S(2)}) %all-to-all-start.4) | async-done | bytes 8388640 | tf_op jit(solution)/shard_map/all_to_all | solution.py:82
  389.6 25.8 %reduce-scatter.3.cloned.1.call-done = f32[128,128]{0,1:T(8,128)} async-done(((f32[128,512]{0,1:T(8,128)}), f32[128,128]{0,1:T(8,128)}) %reduce-scatter.3.cloned.1.call-update) | async-done | bytes 65552 | tf_op jit(solution)/shard_map/reduce_scatter | solution.py:90
  417.4 6.3 add_bitcast_fusion.1
  429.8 7.2 all-to-all-start.5
  439.1 12.1 %all-to-all-done.5 = f32[32,48,128]{2,1,0:T(8,128)S(1)} async-done(((f32[32,48,128]{2,1,0:T(8,128)}), f32[32,48,128]{2,1,0:T(8,128)S(1)}, u32[]{:S(2)}, u32[]{:S(2)}) %all-to-all-start.5) | async-done | bytes 786464 | tf_op jit(solution)/shard_map/all_to_all | solution.py:55
  451.2 9.5 scatter_fusion.1
  471.4 8.5 all-to-all-done.6
  485.7 6.3 convolution_bitcast_fusion.1
  507.4 5.9 all-to-all-done.7
  513.3 10.8 %scatter_fusion.2 = f32[3072,128]{1,0:T(8,128)} fusion(f32[3072,128]{1,0:T(8,128)} %bitcast.126, s32[1536]{0:T(1024)S(1)} %fusion.35, f32[1536,128]{1,0:T(8,128)S(1)} %bitcast.140), kind=kCustom, calls=%fused_computation.16 | custom fusion | flops 196608 | bytes 2365440 | tf_op jit(solution)/shard_map/scatter-add | solution.py:63
  536.8 8.5 all-to-all-done.8
  552.2 149.8 %all-gather.5.cloned.1.call-done = f32[4096,128]{1,0:T(8,128)} async-done(((f32[128,128]{1,0:T(8,128)}), f32[4096,128]{1,0:T(8,128)}) %all-gather.5.cloned.1.call-update) | async-done | bytes 2097168 | tf_op jit(solution)/shard_map/all_gather | solution.py:77
  707.6 98.9 %all_to_all.72 = f32[4,4096,128]{1,2,0:T(8,128)S(1)} all-to-all(f32[4,4096,128]{1,2,0:T(8,128)S(1)} %stack.5), channel_id=1, replica_groups=mesh['wide'=32,'narrow'=4] {'narrow'}, dimensions={0} | all-to-all | bytes 16777216 | tf_op jit(solution)/shard_map/all_to_all | solution.py:82
  809.0 25.3 %reduce-scatter.5.cloned.1.call-done = f32[128,128]{0,1:T(8,128)} async-done(((f32[128,512]{0,1:T(8,128)}), f32[128,128]{0,1:T(8,128)}) %reduce-scatter.5.cloned.1.call-update) | async-done | bytes 65552 | tf_op jit(solution)/shard_map/reduce_scatter | solution.py:90
  836.3 6.3 add_bitcast_fusion
  851.3 7.2 all-to-all-start.10
  861.2 11.5 %all-to-all-done.10 = f32[32,48,128]{2,1,0:T(8,128)S(1)} async-done(((f32[32,48,128]{2,1,0:T(8,128)}), f32[32,48,128]{2,1,0:T(8,128)S(1)}, u32[]{:S(2)}, u32[]{:S(2)}) %all-to-all-start.10) | async-done | bytes 786464 | tf_op jit(solution)/shard_map/all_to_all | solution.py:55
  872.6 10.8 %scatter_fusion.3 = f32[3072,128]{1,0:T(8,128)} fusion(f32[3072,128]{1,0:T(8,128)} %bitcast_add_fusion, s32[1536]{0:T(1024)S(1)} %fusion.35, f32[1536,128]{1,0:T(8,128)S(1)} %bitcast.141), kind=kCustom, calls=%fused_computation.18 | custom fusion | flops 196608 | bytes 2365440 | tf_op jit(solution)/shard_map/scatter-add | solution.py:63
  894.1 9.4 all-to-all-done.11
  907.6 6.4 convolution_bitcast_fusion
  926.6 8.5 all-to-all-done.12
  935.0 9.5 scatter_fusion.4
  (141 shorter events, 175.4 us)
Async XLA Ops:
  7.2 378.3 %copy-start = (f32[128,1024]{1,0:T(8,128)S(1)}, f32[128,1024]{1,0:T(8,128)}, u32[]{:S(2)}) copy-start(f32[128,1024]{1,0:T(8,128)} %param.12) | copy-start | bytes 1572868
  20.3 52.7 %copy-start.12 = (s32[1024,1]{0,1:T(1,128)}, s32[1024,1]{0,1:T(1,128)S(1)}, u32[]{:S(2)}) copy-start(s32[1024,1]{0,1:T(1,128)S(1)} %compare_select_fusion.2) | copy-start | bytes 12292
  25.4 17.0 %all-to-all-start = ((s32[32,1,48]{2,1,0:T(1,128)}), s32[32,1,48]{2,1,0:T(1,128)S(1)}, u32[]{:S(2)}, u32[]{:S(2)}) async-start(s32[32,1,48]{2,1,0:T(1,128)} %all_to_all.44), calls=%async_computation | async-start | bytes 32768 | tf_op jit(solution)/shard_map/all_to_all | solution.py:30
  42.4 65.3 %copy-start.7 = (pred[32,48]{1,0:T(8,128)(4,1)}, pred[32,48]{1,0:T(8,128)(4,1)S(1)}, u32[]{:S(2)}) copy-start(pred[32,48]{1,0:T(8,128)(4,1)S(1)} %compare_bitcast_fusion) | copy-start | bytes 4612
  48.0 13.6 %all-to-all-start.1 = ((bf16[32,48,128]{2,1,0:T(8,128)(2,1)}), bf16[32,48,128]{2,1,0:T(8,128)(2,1)S(1)}, u32[]{:S(2)}, u32[]{:S(2)}) async-start(bf16[32,48,128]{2,1,0:T(8,128)(2,1)} %broadcast_select_fusion.4), calls=%async_computation.1 | async-start | bytes 786432 | tf_op jit(solution)/shard_map/all_to_all | solution.py:39
  52.1 19.8 %copy-start.9 = (s32[1024]{0:T(1024)}, s32[1024]{0:T(1024)S(1)}, u32[]{:S(2)}) copy-start(s32[1024]{0:T(1024)S(1)} %broadcast_clamp_fusion) | copy-start | bytes 12292
  77.4 16.0 %all-to-all-start.2 = ((f32[32,48,128]{2,1,0:T(8,128)}), f32[32,48,128]{2,1,0:T(8,128)S(1)}, u32[]{:S(2)}, u32[]{:S(2)}) async-start(f32[32,48,128]{2,1,0:T(8,128)} %bitcast.144), calls=%async_computation.2 | async-start | bytes 1572864 | tf_op jit(solution)/shard_map/all_to_all | solution.py:55
  107.6 15.2 %copy-start.10 = (s32[1024]{0:T(1024)S(1)}, s32[1024]{0:T(1024)}, u32[]{:S(2)}) copy-start(s32[1024]{0:T(1024)} %copy-done.9) | copy-start | bytes 12292
  108.7 14.1 %all-to-all-start.3 = ((bf16[32,48,128]{2,1,0:T(8,128)(2,1)}), bf16[32,48,128]{2,1,0:T(8,128)(2,1)S(1)}, u32[]{:S(2)}, u32[]{:S(2)}) async-start(bf16[32,48,128]{2,1,0:T(8,128)(2,1)} %broadcast_select_fusion.3), calls=%async_computation.3 | async-start | bytes 786432 | tf_op jit(solution)/shard_map/all_to_all | solution.py:39
  113.1 165.7 %all-gather.3.cloned.1.call-start = ((), (), s32[]{:S(2)}) async-start(), calls=%async_computation.15 | async-start | bytes 2162688 | tf_op jit(solution)/shard_map/all_gather | solution.py:77
  113.3 12.9 %copy-start.6 = (bf16[4,1024,32]{1,2,0:T(8,128)(2,1)S(1)}, bf16[4,1024,32]{1,2,0:T(8,128)(2,1)}, u32[]{:S(2)}) copy-start(bf16[4,1024,32]{1,2,0:T(8,128)(2,1)} %param.11) | copy-start | bytes 786436
  113.6 13.7 %copy-start.3 = (bf16[4,768,128]{1,2,0:T(8,128)(2,1)}, bf16[4,768,128]{1,2,0:T(8,128)(2,1)S(1)}, u32[]{:S(2)}) copy-start(bf16[4,768,128]{1,2,0:T(8,128)(2,1)S(1)} %copy.76) | copy-start | bytes 2359300
  285.1 100.3 %all-to-all-start.4 = ((f32[4,4096,128]{1,2,0:T(8,128)}), f32[4,4096,128]{1,2,0:T(8,128)}, u32[]{:S(2)}, u32[]{:S(2)}) async-start(f32[4,4096,128]{1,2,0:T(8,128)} %stack.4), calls=%async_computation.4 | async-start | bytes 16777216 | tf_op jit(solution)/shard_map/all_to_all | solution.py:82
  290.8 124.6 %reduce-scatter.3.cloned.1.call-start = ((), (), s32[]{:S(2)}) async-start(), calls=%async_computation.16 | async-start | bytes 327680 | tf_op jit(solution)/shard_map/reduce_scatter | solution.py:90
  389.6 27.9 %copy-start.4 = (bf16[4,768,128]{1,2,0:T(8,128)(2,1)S(1)}, bf16[4,768,128]{1,2,0:T(8,128)(2,1)}, u32[]{:S(2)}) copy-start(bf16[4,768,128]{1,2,0:T(8,128)(2,1)} %copy-done.3) | copy-start | bytes 2359300
  429.8 21.4 %all-to-all-start.5 = ((f32[32,48,128]{2,1,0:T(8,128)}), f32[32,48,128]{2,1,0:T(8,128)S(1)}, u32[]{:S(2)}, u32[]{:S(2)}) async-start(f32[32,48,128]{2,1,0:T(8,128)} %bitcast.28), calls=%async_computation.6 | async-start | bytes 1572864 | tf_op jit(solution)/shard_map/all_to_all | solution.py:55
  465.6 14.3 %all-to-all-start.6 = ((bf16[32,48,128]{2,1,0:T(8,128)(2,1)}), bf16[32,48,128]{2,1,0:T(8,128)(2,1)S(1)}, u32[]{:S(2)}, u32[]{:S(2)}) async-start(bf16[32,48,128]{2,1,0:T(8,128)(2,1)} %broadcast_select_fusion.2), calls=%async_computation.7 | async-start | bytes 786432 | tf_op jit(solution)/shard_map/all_to_all | solution.py:39
  471.4 14.3 %copy-start.2 = (bf16[4,768,128]{1,2,0:T(8,128)(2,1)S(1)}, bf16[4,768,128]{1,2,0:T(8,128)(2,1)}, u32[]{:S(2)}) copy-start(bf16[4,768,128]{1,2,0:T(8,128)(2,1)} %copy.83) | copy-start | bytes 2359300
  492.0 1.3 copy-start.1
  497.7 15.6 %all-to-all-start.7 = ((f32[32,48,128]{2,1,0:T(8,128)}), f32[32,48,128]{2,1,0:T(8,128)S(1)}, u32[]{:S(2)}, u32[]{:S(2)}) async-start(f32[32,48,128]{2,1,0:T(8,128)} %bitcast.145), calls=%async_computation.8 | async-start | bytes 1572864 | tf_op jit(solution)/shard_map/all_to_all | solution.py:55
  531.1 14.2 %all-to-all-start.8 = ((bf16[32,48,128]{2,1,0:T(8,128)(2,1)}), bf16[32,48,128]{2,1,0:T(8,128)(2,1)S(1)}, u32[]{:S(2)}, u32[]{:S(2)}) async-start(bf16[32,48,128]{2,1,0:T(8,128)(2,1)} %broadcast_select_fusion.1), calls=%async_computation.9 | async-start | bytes 786432 | tf_op jit(solution)/shard_map/all_to_all | solution.py:39
  535.6 166.4 %all-gather.5.cloned.1.call-start = ((), (), s32[]{:S(2)}) async-start(), calls=%async_computation.17 | async-start | bytes 2162688 | tf_op jit(solution)/shard_map/all_gather | solution.py:77
  536.8 14.2 %copy-start.5 = (bf16[4,768,128]{1,2,0:T(8,128)(2,1)S(1)}, bf16[4,768,128]{1,2,0:T(8,128)(2,1)}, u32[]{:S(2)}) copy-start(bf16[4,768,128]{1,2,0:T(8,128)(2,1)} %copy.87) | copy-start | bytes 2359300
  552.2 282.1 %reduce-scatter.5.cloned.1.call-start = ((), (), s32[]{:S(2)}) async-start(), calls=%async_computation.18 | async-start | bytes 327680 | tf_op jit(solution)/shard_map/reduce_scatter | solution.py:90
  851.3 21.4 %all-to-all-start.10 = ((f32[32,48,128]{2,1,0:T(8,128)}), f32[32,48,128]{2,1,0:T(8,128)S(1)}, u32[]{:S(2)}, u32[]{:S(2)}) async-start(f32[32,48,128]{2,1,0:T(8,128)} %bitcast.146), calls=%async_computation.12 | async-start | bytes 1572864 | tf_op jit(solution)/shard_map/all_to_all | solution.py:55
  884.9 3.2 copy-start.8
  888.1 15.4 %copy-start.11 = (s32[1024]{0:T(1024)S(1)}, s32[1024]{0:T(1024)}, u32[]{:S(2)}) copy-start(s32[1024]{0:T(1024)} %copy-done.9) | copy-start | bytes 12292
  889.2 14.4 %all-to-all-start.11 = ((bf16[32,48,128]{2,1,0:T(8,128)(2,1)}), bf16[32,48,128]{2,1,0:T(8,128)(2,1)S(1)}, u32[]{:S(2)}, u32[]{:S(2)}) async-start(bf16[32,48,128]{2,1,0:T(8,128)(2,1)} %broadcast_select_fusion), calls=%async_computation.13 | async-start | bytes 786432 | tf_op jit(solution)/shard_map/all_to_all | solution.py:39
  919.4 15.6 %all-to-all-start.12 = ((f32[32,48,128]{2,1,0:T(8,128)}), f32[32,48,128]{2,1,0:T(8,128)S(1)}, u32[]{:S(2)}, u32[]{:S(2)}) async-start(f32[32,48,128]{2,1,0:T(8,128)} %bitcast.143), calls=%async_computation.14 | async-start | bytes 1572864 | tf_op jit(solution)/shard_map/all_to_all | solution.py:55
Sparse Core Ops, SparseCore 0:
  127.4 151.3 all-gather.2
  389.7 25.6 reduce-scatter.2
  552.3 149.7 all-gather.4
  809.2 25.0 reduce-scatter.4
